TPU v7x, 32 devices: a whole 2x2x4 slice. The times are simulated.
32 devices in a mesh: grp: 2 (over x), tm: 16 (over z, y, core).
Axes of the slice: x: 2, y: 2, z: 4, core: 2. Of those that a mesh axis runs over, the one named last changes fastest.
Arguments:
- block_input: bfloat16 [4, 16, 120, 384], P('grp', 'tm'), parts along dimension 0, may hold values from -6 to 6
- hidden_state: bfloat16 [4, 16, 120, 384], P('grp', 'tm'), parts along dimension 0, may hold values from -6 to 6
- norm_gain: float32 [384], replicated, may hold values from 0.5 to 1.5
- conv_weight: bfloat16 [3, 3, 3, 384, 384], replicated, may hold values from -0.0625 to 0.0625
- attn_gain: float32 [384], replicated, may hold values from 0.5 to 1.5
- qkv_weight: bfloat16 [384, 1152], replicated, may hold values from -4 to 4
- proj_weight: bfloat16 [384, 384], replicated, may hold values from -0.3125 to 0.3125
Outputs:
- block_output: bfloat16 [4, 16, 120, 384], P('grp', 'tm'), parts along dimension 0
There are 2 independent parts, one for each index of `grp`. A program takes and returns all parts, laid end to end along the dimension named above; an argument that names none is the same for every part. Nothing has to cross between parts.
All inputs are finite; a program needn't handle non-finite values.
Results may differ from a plain program's by a relative error of at most 0.006.
Values may be sent and summed in bfloat16 or wider, within the bound.
A program may use at most 128 MiB of HBM per device.

v0:
```python
import jax
import jax.numpy as jnp
from jax import lax
from jax.sharding import PartitionSpec as P


def with_halo(x, sides, width):
    for axis, dim in sides:
        peers, length = (lax.axis_size(axis), x.shape[dim])
        up = [(i, (i + 1) % peers) for i in range(peers - 1)]
        down = [(j, i) for i, j in up]
        last = lax.slice_in_dim(x, length - width, length, axis=dim)
        leading = lax.slice_in_dim(x, 0, width, axis=dim)
        before = lax.ppermute(last, axis, up)
        after = lax.ppermute(leading, axis, down)
        x = jnp.concatenate([before, x, after], axis=dim)
    return x


def rms_scale(values, gain):
    wide = values.astype(jnp.float32)
    return wide * lax.rsqrt(jnp.mean(wide * wide, axis=-1, keepdims=True) + 1e-06) * gain


def causal_conv(padded, kernel):
    channels = padded.shape[-1]
    frames = padded.shape[0] - 2
    row_count = padded.shape[1] - 2
    col_count = padded.shape[2] - 2
    pieces = [
        padded[t_off : t_off + frames, r_off : r_off + row_count, c_off : c_off + col_count, :]
        for t_off in range(3)
        for r_off in range(3)
        for c_off in range(3)
    ]
    stacked = jnp.concatenate(pieces, axis=-1).reshape(-1, 27 * channels)
    result = jnp.dot(
        stacked, kernel.reshape(27 * channels, channels), preferred_element_type=jnp.float32
    )
    return result.reshape(frames, row_count, col_count, channels)


def attend(queries, key_value, mixed_frame, proj_weight):
    channels = queries.shape[-1]
    key_part = key_value[:, :channels]
    value_part = key_value[:, channels:]
    scores = jnp.dot(queries, key_part.T, preferred_element_type=jnp.float32) * channels ** (-0.5)
    scores = scores - jnp.max(scores, axis=-1, keepdims=True)
    expo = jnp.exp(scores)
    weights = (expo / jnp.sum(expo, axis=-1, keepdims=True)).astype(jnp.bfloat16)
    attended = jnp.dot(weights, value_part, preferred_element_type=jnp.float32).astype(jnp.bfloat16)
    result = mixed_frame.reshape(-1, channels).astype(jnp.float32) + jnp.dot(
        attended, proj_weight, preferred_element_type=jnp.float32
    )
    return result.astype(jnp.bfloat16).reshape(mixed_frame.shape)


def body(block_input, hidden_state, norm_gain, conv_weight, attn_gain, qkv_weight, proj_weight):
    channels = block_input.shape[-1]
    frames = block_input.shape[0]
    conv_in = jax.nn.silu(rms_scale(hidden_state, norm_gain)).astype(jnp.bfloat16)
    padded = with_halo(conv_in, (("tm", 1),), 1)
    padded = jnp.pad(padded, ((2, 0), (0, 0), (1, 1), (0, 0)))
    conv_out = causal_conv(padded, conv_weight)
    mixed = (block_input.astype(jnp.float32) + conv_out).astype(jnp.bfloat16)
    normed = rms_scale(mixed, attn_gain).astype(jnp.bfloat16)
    local_rows = normed.shape[1] * normed.shape[2]
    projected = jnp.dot(
        normed.reshape(-1, channels), qkv_weight, preferred_element_type=jnp.float32
    ).astype(jnp.bfloat16)
    queries = projected[:, :channels].reshape(frames, local_rows, channels)
    key_value = projected[:, channels:].reshape(
        frames, normed.shape[1], normed.shape[2], 2 * channels
    )
    whole = lax.all_gather(key_value, "tm", axis=1, tiled=True)
    whole = whole.reshape(frames, -1, 2 * channels)
    return lax.map(
        lambda triple: attend(triple[0], triple[1], triple[2], proj_weight), (queries, whole, mixed)
    )


def solution(mesh):
    return jax.shard_map(
        body,
        mesh=mesh,
        in_specs=(P("grp", "tm", None, None), P("grp", "tm", None, None), P(), P(), P(), P(), P()),
        out_specs=P("grp", "tm", None, None),
        check_vma=False,
    )
```

profile of v0, /device:TPU:0, one launch (start us, length us, event | category | flops | bytes accessed | tf_op | source)
XLA Modules:
  0.0 113.6 jit_solution(8456333361618802162)
XLA Ops:
  6.5 0.0 copy-start
  6.5 0.0 copy-start.2
  6.5 0.0 copy-start.4
  6.5 0.0 all-gather.2.cloned.1.call-start
  6.5 1.1 fusion.44
  7.7 1.1 fusion.51
  8.8 0.0 copy-start.6
  8.8 0.0 copy-start.8
  8.8 1.6 %collective-permute-start.1 = (bf16[2,1,120,384]{3,2,0,1:T(8,128)(2,1)S(1)}, bf16[2,1,120,384]{3,2,0,1:T(8,128)(2,1)S(1)}, u32[]{:S(2)}, u32[]{:S(2)}) collective-permute-start(bf16[2,1,120,384]{3,2,0,1:T(8,128)(2,1)S(1)} %fusion.51), channel_id=1, source_target_pairs={{1,0},{2,1},{3,2},{4,3},{5,4},{6,5},{7,6},{8,7},{9,8},{10,9},{11,1... | collective-permute-start | bytes 552968 | tf_op jit(solution)/shard_map/ppermute | solution.py:15
  10.4 3.2 %collective-permute-start = (bf16[2,1,120,384]{3,2,0,1:T(8,128)(2,1)S(1)}, bf16[2,1,120,384]{3,2,0,1:T(8,128)(2,1)S(1)}, u32[]{:S(2)}, u32[]{:S(2)}) collective-permute-start(bf16[2,1,120,384]{3,2,0,1:T(8,128)(2,1)S(1)} %fusion.51), channel_id=1, source_target_pairs={{0,1},{1,2},{2,3},{3,4},{4,5},{5,6},{6,7},{7,8},{8,9},{9,10},{10,1... | collective-permute-start | bytes 552968 | tf_op jit(solution)/shard_map/ppermute | solution.py:14
  13.9 0.0 collective-permute-done.1
  13.9 0.7 collective-permute-done
  14.6 0.2 fusion.35
  14.8 0.1 slice_dynamic-update-slice_fusion.13
  14.9 0.1 slice_dynamic-update-slice_fusion.12
  15.0 0.1 slice_dynamic-update-slice_fusion.10
  15.1 0.1 slice_dynamic-update-slice_fusion.9
  15.2 0.1 slice_dynamic-update-slice_fusion.7
  15.2 0.1 slice_dynamic-update-slice_fusion.6
  15.4 0.1 slice_dynamic-update-slice_fusion.4
  15.5 0.0 copy-done.2
  15.5 0.0 copy-done.4
  15.5 0.2 constant_dynamic-update-slice_fusion.1
  15.7 0.1 slice_dynamic-update-slice_fusion.2
  15.9 0.1 slice_dynamic-update-slice_fusion
  15.9 0.0 copy-done.6
  15.9 0.0 copy-done.8
  15.9 0.0 copy-start.5
  16.0 3.0 %fusion.52 = (f32[2,120]{1,0:T(2,128)S(1)}, bf16[2,1,120,384]{3,2,0,1:T(8,128)(2,1)S(1)}) fusion(bf16[10368,384,1]{1,0,2:T(8,128)(2,1)S(1)} %bitcast.67, bf16[2,1,120,10368]{3,2,0,1:T(8,128)(2,1)S(1)} %slice_dynamic-update-slice_fusion, bf16[2,1,120,384]{3,2,1,0:T(8,128)(2,1)S(1)} %copy-done.8), kind=kOutput, calls=%fused_computation.49 | convolution fusion | flops 1911582464 | bytes 13308864 | tf_op jit(solution)/shard_map/dot_general | solution.py:37
  19.0 0.0 copy-done.5
  19.0 0.1 fusion.54
  19.1 0.0 copy-done
  19.1 0.5 convolution_convert_fusion
  19.6 0.8 slice.107
  20.4 0.0 all-gather.2.cloned.1.call-update
  20.4 0.0 copy-start.7
  20.4 66.2 %all-gather.2.cloned.1.call-done = bf16[2,16,120,768]{3,2,0,1:T(8,128)(2,1)} async-done(((bf16[2,1,120,768]{3,2,0,1:T(8,128)(2,1)}), bf16[2,16,120,768]{3,2,0,1:T(8,128)(2,1)}) %all-gather.2.cloned.1.call-update) | async-done | bytes 5898256 | tf_op jit(solution)/shard_map/all_gather | solution.py:75
  86.6 5.6 %copy.19 = bf16[2,16,120,768]{3,2,1,0:T(8,128)(2,1)} copy(bf16[2,16,120,768]{3,2,0,1:T(8,128)(2,1)} %all-gather.2.cloned.1.call-done) | data formatting | bytes 11796480 | tf_op jit(solution)/shard_map/all_gather | solution.py:75
  92.2 0.0 copy-done.7
  92.2 13.8 %while.10 = (s32[]{:T(128)}, bf16[2,1,120,384]{3,2,1,0:T(8,128)(2,1)S(1)}, bf16[2,1,120,384]{3,2,1,0:T(8,128)(2,1)S(1)}, bf16[2,120,384]{2,1,0:T(8,128)(2,1)S(1)...) while((s32[]{:T(128)}, bf16[2,1,120,384]{3,2,1,0:T(8,128)(2,1)S(1)}, ...), condition=%wide.region_5.6_spmd, body=%wide.region_2.5_spmd.sunk | while | flops 391080704 | bytes 23982620 | solution.py:77
  92.2 2.0 %dynamic-slice_bitcast_fusion.2 = bf16[1920,768]{1,0:T(8,128)(2,1)S(1)} fusion(bf16[2,1920,768]{2,1,0:T(8,128)(2,1)} %get-tuple-element.131, s32[]{:T(128)S(6)} %copy.51), kind=kLoop, calls=%fused_computation.clone.1 | loop fusion | bytes 5898244 | tf_op jit(solution)/shard_map/while/body/jit(dynamic_index_in_dim)/squeeze | solution.py:77
  94.2 0.0 copy-start.1
  94.2 1.6 %copy-done.1 = bf16[1920,768]{1,0:T(8,128)(2,1)} copy-done((bf16[1920,768]{1,0:T(8,128)(2,1)}, bf16[1920,768]{1,0:T(8,128)(2,1)S(1)}, u32[]{:S(2)}) %copy-start.1) | copy-done | bytes 2949144 | tf_op jit(solution)/shard_map/while
  95.9 0.9 fusion.67
  96.7 0.3 fusion.68
  97.0 2.1 %fusion.69 = bf16[2,1,120,384]{3,2,1,0:T(8,128)(2,1)S(1)} fusion(bf16[2,1,120,384]{3,2,1,0:T(8,128)(2,1)S(1)} %get-tuple-element.121, s32[]{:T(128)S(6)} %copy.51, bf16[384,384]{1,0:T(8,128)(2,1)S(1)} %get-tuple-element.132, bf16[1920,768]{1,0:T(8,128)(2,1)} %copy-done.1, f32[120,1920]{1,0:T(8,128)S(1)} %get-tuple-element.111, f32[120]{0:T(128)S(1)} %fusion.68, ...), kind=kOutput, calls=%fused_computation.9.clone.1 | convolution fusion | flops 213212160 | bytes 2876420 | tf_op jit(solution)/shard_map/while/body/eval_jaxpr/dot_general | solution.py:52
  99.1 2.0 %dynamic-slice_bitcast_fusion.2 = bf16[1920,768]{1,0:T(8,128)(2,1)S(1)} fusion(bf16[2,1920,768]{2,1,0:T(8,128)(2,1)} %get-tuple-element.131, s32[]{:T(128)S(6)} %copy.51), kind=kLoop, calls=%fused_computation.clone.1 | loop fusion | bytes 5898244 | tf_op jit(solution)/shard_map/while/body/jit(dynamic_index_in_dim)/squeeze | solution.py:77
  101.1 0.0 copy-start.1
  101.2 1.6 %copy-done.1 = bf16[1920,768]{1,0:T(8,128)(2,1)} copy-done((bf16[1920,768]{1,0:T(8,128)(2,1)}, bf16[1920,768]{1,0:T(8,128)(2,1)S(1)}, u32[]{:S(2)}) %copy-start.1) | copy-done | bytes 2949144 | tf_op jit(solution)/shard_map/while
  102.8 0.9 fusion.67
  103.7 0.3 fusion.68
  104.0 2.1 %fusion.69 = bf16[2,1,120,384]{3,2,1,0:T(8,128)(2,1)S(1)} fusion(bf16[2,1,120,384]{3,2,1,0:T(8,128)(2,1)S(1)} %get-tuple-element.121, s32[]{:T(128)S(6)} %copy.51, bf16[384,384]{1,0:T(8,128)(2,1)S(1)} %get-tuple-element.132, bf16[1920,768]{1,0:T(8,128)(2,1)} %copy-done.1, f32[120,1920]{1,0:T(8,128)S(1)} %get-tuple-element.111, f32[120]{0:T(128)S(1)} %fusion.68, ...), kind=kOutput, calls=%fused_computation.9.clone.1 | convolution fusion | flops 213212160 | bytes 2876420 | tf_op jit(solution)/shard_map/while/body/eval_jaxpr/dot_general | solution.py:52
  106.0 0.0 copy-start.3
  106.1 0.7 copy-done.3
  (21 shorter events, 0.6 us)
Async XLA Ops:
  6.5 12.6 %copy-start = (bf16[384,1152]{1,0:T(8,128)(2,1)S(1)}, bf16[384,1152]{1,0:T(8,128)(2,1)}, u32[]{:S(2)}) copy-start(bf16[384,1152]{1,0:T(8,128)(2,1)} %param.14) | copy-start | bytes 2654212
  6.5 9.0 %copy-start.2 = (bf16[2,1,120,384]{3,2,1,0:T(8,128)(2,1)S(1)}, bf16[2,1,120,384]{3,2,1,0:T(8,128)(2,1)}, u32[]{:S(2)}) copy-start(bf16[2,1,120,384]{3,2,1,0:T(8,128)(2,1)} %param.10) | copy-start | bytes 552964
  6.5 9.0 %copy-start.4 = (f32[384]{0:T(512)S(1)}, f32[384]{0:T(512)}, u32[]{:S(2)}) copy-start(f32[384]{0:T(512)} %param.11) | copy-start | bytes 4612
  6.5 80.1 %all-gather.2.cloned.1.call-start = ((), (), s32[]{:S(2)}) async-start(), calls=%async_computation | async-start | bytes 6266880 | tf_op jit(solution)/shard_map/all_gather | solution.py:75
  8.8 7.1 %copy-start.6 = (bf16[3,3,3,384,384]{4,3,2,1,0:T(8,128)(2,1)S(1)}, bf16[3,3,3,384,384]{4,3,2,1,0:T(8,128)(2,1)}, u32[]{:S(2)}) copy-start(bf16[3,3,3,384,384]{4,3,2,1,0:T(8,128)(2,1)} %param.12) | copy-start | bytes 23887876
  8.8 7.1 %copy-start.8 = (bf16[2,1,120,384]{3,2,1,0:T(8,128)(2,1)S(1)}, bf16[2,1,120,384]{3,2,1,0:T(8,128)(2,1)}, u32[]{:S(2)}) copy-start(bf16[2,1,120,384]{3,2,1,0:T(8,128)(2,1)} %param.9) | copy-start | bytes 552964
  8.8 5.0 %collective-permute-start.1 = (bf16[2,1,120,384]{3,2,0,1:T(8,128)(2,1)S(1)}, bf16[2,1,120,384]{3,2,0,1:T(8,128)(2,1)S(1)}, u32[]{:S(2)}, u32[]{:S(2)}) collective-permute-start(bf16[2,1,120,384]{3,2,0,1:T(8,128)(2,1)S(1)} %fusion.51), channel_id=1, source_target_pairs={{1,0},{2,1},{3,2},{4,3},{5,4},{6,5},{7,6},{8,7},{9,8},{10,9},{11,1... | collective-permute-start | bytes 552968 | tf_op jit(solution)/shard_map/ppermute | solution.py:15
  10.4 4.2 %collective-permute-start = (bf16[2,1,120,384]{3,2,0,1:T(8,128)(2,1)S(1)}, bf16[2,1,120,384]{3,2,0,1:T(8,128)(2,1)S(1)}, u32[]{:S(2)}, u32[]{:S(2)}) collective-permute-start(bf16[2,1,120,384]{3,2,0,1:T(8,128)(2,1)S(1)} %fusion.51), channel_id=1, source_target_pairs={{0,1},{1,2},{2,3},{3,4},{4,5},{5,6},{6,7},{7,8},{8,9},{9,10},{10,1... | collective-permute-start | bytes 552968 | tf_op jit(solution)/shard_map/ppermute | solution.py:14
  15.9 3.0 %copy-start.5 = (f32[384]{0:T(512)S(1)}, f32[384]{0:T(512)}, u32[]{:S(2)}) copy-start(f32[384]{0:T(512)} %param.13) | copy-start | bytes 4612
  20.4 71.8 %copy-start.7 = (bf16[384,384]{1,0:T(8,128)(2,1)S(1)}, bf16[384,384]{1,0:T(8,128)(2,1)}, u32[]{:S(2)}) copy-start(bf16[384,384]{1,0:T(8,128)(2,1)} %param.15) | copy-start | bytes 884740
  94.2 1.7 %copy-start.1 = (bf16[1920,768]{1,0:T(8,128)(2,1)}, bf16[1920,768]{1,0:T(8,128)(2,1)S(1)}, u32[]{:S(2)}) copy-start(bf16[1920,768]{1,0:T(8,128)(2,1)S(1)} %dynamic-slice_bitcast_fusion.2) | copy-start | bytes 8847364 | tf_op jit(solution)/shard_map/while
  101.1 1.7 %copy-start.1 = (bf16[1920,768]{1,0:T(8,128)(2,1)}, bf16[1920,768]{1,0:T(8,128)(2,1)S(1)}, u32[]{:S(2)}) copy-start(bf16[1920,768]{1,0:T(8,128)(2,1)S(1)} %dynamic-slice_bitcast_fusion.2) | copy-start | bytes 8847364 | tf_op jit(solution)/shard_map/while
  106.0 0.7 copy-start.3
Sparse Core Ops, SparseCore 0:
  20.5 66.0 all-gather.1
where the time goes:
time: 114 us
  waiting for transfers between devices  66.9 us (59%)
  local copies, waits for them, and re-layouts  15.5 us (14%)
  between operations  13.7 us (12%)
  matrix products  9.36 us (8%)
  starting transfers between devices  4.73 us (4%)
  other arithmetic  3.35 us (3%)
    all_gather x1, waiting for transfers between devices, body(): whole = lax.all_gather(key_value, 'tm', axis=1, tiled=True)  66.2 us
    all_gather x1, local copies, waits for them, and re-layouts, body(): whole = lax.all_gather(key_value, 'tm', axis=1, tiled=True)  5.57 us
    dot_general x2, matrix products, attend(): jnp.dot(attended, proj_weight, preferred_element_type=jnp.float32)  4.14 us
    squeeze x2, local copies, waits for them, and re-layouts, body(): lax.map(lambda triple: attend(triple[0], triple[1], triple[2], proj_weigh...  4.05 us
    while x4, local copies, waits for them, and re-layouts  3.29 us
    ppermute x1, starting transfers between devices, with_halo(): before = lax.ppermute(last, axis, up)  3.17 us
    dot_general x1, matrix products, causal_conv(): jnp.dot(stacked, kernel.reshape(27 * channels, channels), preferred_eleme...  2.99 us
  transfers between devices with their start and end apart: 3, of which 2 were waited for; matrix products, arithmetic and copies ran while one was open for 0% of the time, Pallas kernels for 0%

commit v1 on v0

v1 whole, which is shorter than its diff:
```python
import functools

import jax
import jax.numpy as jnp
from jax import lax
from jax.experimental import pallas as pl
from jax.experimental.pallas import tpu as pltpu
from jax.sharding import PartitionSpec as P

MESH = pl.DeviceIdType.MESH
BF16 = jnp.bfloat16
F32 = jnp.float32
SLOT = 128
EPS = 1e-06


def mm(a, b):
    return jnp.dot(a, b, preferred_element_type=F32)


def mm_t(a, b):
    return lax.dot_general(a, b, (((1,), (1,)), ((), ())), preferred_element_type=F32)


def rms(wide, gain):
    return wide * lax.rsqrt(jnp.mean(wide * wide, axis=-1, keepdims=True) + EPS) * gain


def kernel(
    n, depth, hid, bi, ng, ag, cw, qkvw, projw, out,
    hal, biv, wv, qkv, proj, x2, acc, mixed, xbuf, gath, oacc, abuf, arecv,
    in_sem, w_sem, halo_send, halo_recv, pair_send, pair_recv, ring_send, ring_recv,
):
    cols, channels = hid.shape[2], hid.shape[3]
    chips = n // 2
    half = chips // 2
    me = lax.axis_index("tm")
    core, chip = me % 2, me // 2
    partner = me + 1 - 2 * core

    def to_pos(c):
        if depth == 1:
            return c
        z, y = c // 2, c % 2
        return z + y * (chips - 1 - 2 * z)

    def to_dev(p):
        if depth == 1:
            return 2 * p + core
        y = p // (chips // 2)
        z = p + y * (chips - 1 - 2 * p)
        return 2 * (2 * z + y) + core

    pos = to_pos(chip)
    right, left = to_dev((pos + 1) % chips), to_dev((pos + chips - 1) % chips)

    loads = [
        pltpu.make_async_copy(hid.at[:, 0], hal.at[1], in_sem.at[0]),
        pltpu.make_async_copy(bi.at[:, 0], biv, in_sem.at[1]),
        pltpu.make_async_copy(qkvw, qkv, in_sem.at[2]),
        pltpu.make_async_copy(projw, proj, in_sem.at[3]),
    ]
    loads[0].start()
    taps = {}
    for b in (1, 0, 2):
        for a in range(2):
            for e in range(3):
                taps[b, a, e] = pltpu.make_async_copy(
                    cw.at[2 - a, b, e],
                    wv.at[b, pl.ds(a * channels, channels), pl.ds(e * channels, channels)],
                    w_sem.at[b, a, e],
                )
    for e in range(3):
        taps[1, 0, e].start()
        taps[1, 1, e].start()
    for copy in loads[1:]:
        copy.start()

    tail = SLOT - 16
    gath[:, :, tail:, :] = jnp.zeros((chips, 2, 16, channels), BF16)

    @pl.when(me == 0)
    def _():
        hal[0] = jnp.zeros(hal.shape[1:], BF16)

    @pl.when(me == n - 1)
    def _():
        hal[2] = jnp.zeros(hal.shape[1:], BF16)

    barrier = pltpu.get_barrier_semaphore()

    def greet(d):
        pl.semaphore_signal(barrier, inc=1, device_id={"tm": d}, device_id_type=MESH)

    across = me - 1 + 2 * core
    inside = jnp.logical_and(across >= 0, across < n)
    greet(partner)
    greet(right)
    greet(left)

    @pl.when(inside)
    def _():
        greet(across)

    has_across = core * ((2 * n - 2 - me) // n) + (1 - core) * ((me + n - 1) // n)
    pl.semaphore_wait(barrier, 3 + has_across)

    def remote(src, dst, send, recv, d):
        return pltpu.make_async_remote_copy(
            src_ref=src, dst_ref=dst, send_sem=send, recv_sem=recv,
            device_id={"tm": d}, device_id_type=MESH,
        )

    down = remote(hid.at[:, 0], hal.at[0], halo_send.at[0], halo_recv.at[0], me + 1)
    up = remote(hid.at[:, 0], hal.at[2], halo_send.at[1], halo_recv.at[1], me - 1)

    @pl.when(me < n - 1)
    def _():
        down.start()

    @pl.when(me > 0)
    def _():
        up.start()

    for b in (0, 2):
        for e in range(3):
            taps[b, 0, e].start()
            taps[b, 1, e].start()

    gain = ng[...]

    def tap_row(b, first):
        wide = hal[b].astype(F32).reshape(2 * cols, channels)
        scaled = rms(wide, gain)
        act = scaled / (1.0 + jnp.exp(-scaled))
        x2[:, :channels] = act.astype(BF16)
        earlier = jnp.concatenate([jnp.zeros((cols, channels), F32), act[:cols]], axis=0)
        x2[:, channels:] = earlier.astype(BF16)
        for a in range(2):
            for e in range(3):
                taps[b, a, e].wait()
        part = mm(x2[...], wv[b])
        if first:
            acc[...] = part
        else:
            acc[...] += part

    loads[0].wait()
    tap_row(1, True)

    @pl.when(me > 0)
    def _():
        down.wait_recv()

    tap_row(0, False)

    @pl.when(me < n - 1)
    def _():
        up.wait_recv()

    tap_row(2, False)

    place = lax.broadcasted_iota(jnp.int32, (2 * cols, channels), 0)
    place = jnp.where(place >= cols, place - cols, place)
    before = pltpu.roll(acc[:, :channels], 1, 0)
    after = pltpu.roll(acc[:, 2 * channels :], 2 * cols - 1, 0)
    conv = acc[:, channels : 2 * channels]
    conv = conv + jnp.where(place == 0, 0.0, before)
    conv = conv + jnp.where(place == cols - 1, 0.0, after)
    loads[1].wait()
    total = biv[...].astype(F32).reshape(2 * cols, channels) + conv
    total = total.astype(BF16).astype(F32)
    mixed[...] = total.reshape(2, cols, channels)
    normed = rms(total, ag[...])
    is_first = core == 0
    mine = jnp.where(is_first, normed[:cols], normed[cols:]).astype(BF16)
    other = jnp.where(is_first, normed[cols:], normed[:cols]).astype(BF16)
    span = pl.ds(0, cols)
    xbuf[...] = other
    swap = remote(
        xbuf, gath.at[pos, core, span], pair_send.at[0], pair_recv.at[0], partner
    )
    swap.start()
    gath[pos, core, :cols, :] = mine

    rows = (core, 1 - core)

    def ring(way, s, j):
        owner = (pos - (s - 1) + chips) % chips if way == 0 else (pos + s - 1) % chips
        slot = gath.at[owner, rows[j], span]
        return remote(
            slot, slot, ring_send.at[way, s - 1, j], ring_recv.at[way, s - 1, j],
            right if way == 0 else left,
        )

    def carried(way, s, j):
        return s < half or (s == half and j == way)

    started = []

    def push(way, s, j):
        if s <= half and carried(way, s, j):
            copy = ring(way, s, j)
            copy.start()
            started.append(copy)

    push(0, 1, 0)
    push(1, 1, 0)
    swap.wait_recv()
    push(0, 1, 1)
    push(1, 1, 1)

    loads[2].wait()
    tokens = gath[pos].reshape(2 * SLOT, channels)
    queries = mm(tokens, qkv[:, :channels]).astype(BF16)
    folded = mm_t(queries, qkv[:, channels : 2 * channels]).astype(BF16)
    key_at = lax.broadcasted_iota(jnp.int32, (1, 2 * SLOT), 1) % SLOT
    bias = jnp.where(key_at < cols, 0.0, -1e30).astype(F32)
    scale = channels ** (-0.5)

    def unit(owner, state):
        block = gath[owner].reshape(2 * SLOT, channels)
        scores = mm_t(folded, block) * scale + bias
        top = jnp.max(scores, axis=-1, keepdims=True)
        if state is None:
            expo = jnp.exp(scores - top)
            oacc[...] = mm(expo.astype(BF16), block)
            return top, jnp.sum(expo, axis=-1, keepdims=True)
        old, mass = state
        top = jnp.maximum(old, top)
        fade = jnp.exp(old - top)
        expo = jnp.exp(scores - top)
        oacc[...] = oacc[...] * fade + mm(expo.astype(BF16), block)
        return top, mass * fade + jnp.sum(expo, axis=-1, keepdims=True)

    state = unit(pos, None)
    for s in range(1, half + 1):
        for j in range(2):
            for way in range(2):
                if carried(way, s, j):
                    ring(way, s, j).wait_recv()
                    push(way, s + 1, j)
        state = unit((pos - s + chips) % chips, state)
        if s < half:
            state = unit((pos + s) % chips, state)

    pooled = (oacc[...] / state[1]).astype(BF16)
    attended = mm(pooled, qkv[:, 2 * channels :])
    low, high = attended[:cols], attended[SLOT : SLOT + cols]
    abuf[...] = jnp.where(is_first, high, low).astype(BF16)
    back = remote(abuf, arecv, pair_send.at[1], pair_recv.at[1], partner)
    back.start()
    loads[3].wait()
    own = jnp.where(is_first, low, high).astype(BF16)
    out[core, 0] = (mixed[core] + mm(own, proj[...])).astype(BF16)
    back.wait_recv()
    out[1 - core, 0] = (mixed[1 - core] + mm(arecv[...], proj[...])).astype(BF16)

    @pl.when(me < n - 1)
    def _():
        down.wait_send()

    @pl.when(me > 0)
    def _():
        up.wait_send()

    swap.wait_send()
    back.wait_send()
    for copy in started:
        copy.wait_send()


def body(n, depth, block_input, hidden_state, norm_gain, conv_weight, attn_gain, qkv_weight, proj_weight):
    frames, _, cols, channels = block_input.shape
    chips = n // 2
    any_spec = pl.BlockSpec(memory_space=pl.ANY)
    vmem_spec = pl.BlockSpec(memory_space=pltpu.VMEM)
    dma = pltpu.SemaphoreType.DMA
    return pl.pallas_call(
        functools.partial(kernel, n, depth),
        out_shape=jax.ShapeDtypeStruct(block_input.shape, BF16),
        in_specs=[any_spec, any_spec, vmem_spec, vmem_spec, any_spec, any_spec, any_spec],
        out_specs=vmem_spec,
        scratch_shapes=[
            pltpu.VMEM((3, frames, cols, channels), BF16),
            pltpu.VMEM((frames, cols, channels), BF16),
            pltpu.VMEM((3, 2 * channels, 3 * channels), BF16),
            pltpu.VMEM((channels, 3 * channels), BF16),
            pltpu.VMEM((channels, channels), BF16),
            pltpu.VMEM((frames * cols, 2 * channels), BF16),
            pltpu.VMEM((frames * cols, 3 * channels), F32),
            pltpu.VMEM((frames, cols, channels), F32),
            pltpu.VMEM((cols, channels), BF16),
            pltpu.VMEM((chips, 2, SLOT, channels), BF16),
            pltpu.VMEM((2 * SLOT, channels), F32),
            pltpu.VMEM((cols, channels), BF16),
            pltpu.VMEM((cols, channels), BF16),
            dma((4,)),
            dma((3, 2, 3)),
            dma((2,)),
            dma((2,)),
            dma((2,)),
            dma((2,)),
            dma((2, chips // 2, 2)),
            dma((2, chips // 2, 2)),
        ],
        compiler_params=pltpu.CompilerParams(
            collective_id=0, has_side_effects=True, vmem_limit_bytes=56 * 1024 * 1024
        ),
    )(
        hidden_state, block_input, norm_gain.reshape(1, -1), attn_gain.reshape(1, -1),
        conv_weight, qkv_weight, proj_weight,
    )


def solution(mesh):
    n = mesh.shape["tm"]
    depth = 2 if mesh.shape["grp"] == 2 else 1
    return jax.shard_map(
        functools.partial(body, n, depth),
        mesh=mesh,
        in_specs=(P("grp", "tm", None, None), P("grp", "tm", None, None), P(), P(), P(), P(), P()),
        out_specs=P("grp", "tm", None, None),
        check_vma=False,
    )
```

time: 114 us -> 37.7 us (0.33)
  waiting for transfers between devices: 66.9 us -> 0 us
  Pallas kernels: 0 us -> 33.3 us
  between operations: 13.7 us -> 0.01 us
  local copies, waits for them, and re-layouts: 15.5 us -> 4.12 us
  matrix products: 9.36 us -> 0 us
  starting transfers between devices: 4.73 us -> 0 us
  other arithmetic: 3.35 us -> 0 us
    all_gather x1 -> x0, waiting for transfers between devices: 66.2 us -> none  [body(): whole = lax.all_gather(key_value, 'tm', axis=1, tiled=True)]
    pallas_call x0 -> x1, Pallas kernels: none -> 33.3 us  [body(): pl.pallas_call(functools.partial(kernel, n, depth), out_shape=jax.ShapeDt...]
    dot_general x6 -> x0, matrix products: 9.36 us -> none  [the longest x2 4.14 us: attend(): jnp.dot(attended, proj_weight, preferred_element_type=jnp.float32)]
    all_gather x1 -> x0, local copies, waits for them, and re-layouts: 5.57 us -> none  [body(): whole = lax.all_gather(key_value, 'tm', axis=1, tiled=True)]
    ppermute x2 -> x0, starting transfers between devices: 4.73 us -> none  [the longest x1 3.17 us: with_halo(): before = lax.ppermute(last, axis, up)]
    squeeze x2 -> x0, local copies, waits for them, and re-layouts: 4.05 us -> none  [body(): lax.map(lambda triple: attend(triple[0], triple[1], triple[2], proj_weigh...]
    while x5 -> x0, local copies, waits for them, and re-layouts: 3.31 us -> none
    reshape x0 -> x2, local copies, waits for them, and re-layouts: none -> 2.5 us  [the longest x1 1.26 us: body(): attn_gain.reshape(1, -1)]
  transfers between devices with their start and end apart: 3 -> 0, of which waited for: 2 -> 0; matrix products, arithmetic and copies ran while one was open for 0% -> 0% of each run, Pallas kernels for 0% -> 0%
where the time goes in v1:
time: 37.7 us; the launch traced here: 37.4 us
  Pallas kernels  33.3 us (88%)
  local copies, waits for them, and re-layouts  4.12 us (11%)
    pallas_call x1, Pallas kernels, body(): pl.pallas_call(functools.partial(kernel, n, depth), out_shape=jax.ShapeDt...  33.3 us
    unnamed x1, local copies, waits for them, and re-layouts  1.61 us
    reshape x1, local copies, waits for them, and re-layouts, body(): attn_gain.reshape(1, -1)  1.26 us
    reshape x1, local copies, waits for them, and re-layouts, body(): norm_gain.reshape(1, -1)  1.24 us

profile of v1, /device:TPU:0, one launch (start us, length us, event | category | flops | bytes accessed | tf_op | source)
XLA Modules:
  0.0 37.4 jit_solution(9546931024253407109)
XLA Ops:
  0.0 1.2 %reshape.6.ng = f32[1,384]{1,0:T(1,128)} reshape(f32[384]{0:T(512)} %param.9) | data formatting | bytes 3072 | tf_op jit(solution)/shard_map/reshape | solution.py:311
  1.2 1.3 %reshape.7.ag = f32[1,384]{1,0:T(1,128)} reshape(f32[384]{0:T(512)} %param.11) | data formatting | bytes 3072 | tf_op jit(solution)/shard_map/reshape | solution.py:311
  2.5 33.3 %shard_map.73 = bf16[2,1,120,384]{3,2,1,0:T(8,128)(2,1)} custom-call(bf16[2,1,120,384]{3,2,1,0:T(8,128)(2,1)} %hid.1, bf16[2,1,120,384]{3,2,1,0:T(8,128)(2,1)} %bi.1, f32[1,384]{1,0:T(1,128)} %reshape.6.ng, f32[1,384]{1,0:T(1,128)} %reshape.7.ag, bf16[3,3,3,384,384]{4,3,2,1,0:T(8,128)(2,1)} %cw.1, bf16[384,1152]{1,0:T(8,128)(2,1)} %qkvw.1, ...), custom_call_target="tpu_custom_call" | custom-call | tf_op jit(solution)/shard_map/pallas_call | solution.py:279
  35.8 1.6 %copy.9 = bf16[2,1,120,384]{3,2,1,0:T(8,128)(2,1)} copy(bf16[2,1,120,384]{3,2,1,0:T(8,128)(2,1)} %shard_map.73) | data formatting | bytes 368640
